TPU v7x, 1024 devices: a whole 4x8x16 slice. The times are simulated.
1024 devices in a mesh: dp: 16 (over y, core), expert: 64 (over z, x).
Axes of the slice: x: 4, y: 8, z: 16, core: 2. Of those that a mesh axis runs over, the one named last changes fastest.
Arguments:
- tokens: bfloat16 [512, 4096], P('expert', 'dp'), may hold values from -6 to 6
- expert_ids: int32 [512, 8], P('expert'), may hold values from 0 to 63, all different within a row; in each aligned block of 8 rows (0 to 7, 8 to 15, ...) at most 3 rows name the same one
- route_weights: float32 [512, 8], P('expert'), may hold values from 0.2 to 1
- w_gate: bfloat16 [64, 4096, 768], P('expert', 'dp'), may hold values from -0.09375 to 0.09375
- w_up: bfloat16 [64, 4096, 768], P('expert', 'dp'), may hold values from -0.09375 to 0.09375
- w_down: bfloat16 [64, 768, 4096], P('expert', None, 'dp'), may hold values from -0.21875 to 0.21875
- grad_out: bfloat16 [512, 4096], P('expert', 'dp'), may hold values from -6 to 6
Outputs:
- layer_out: bfloat16 [512, 4096], P('expert', 'dp')
- input_grad: bfloat16 [512, 4096], P('expert', 'dp')
- gate_weight_grad: bfloat16 [64, 4096, 768], P('expert', 'dp')
- up_weight_grad: bfloat16 [64, 4096, 768], P('expert', 'dp')
- down_weight_grad: bfloat16 [64, 768, 4096], P('expert', None, 'dp')
Inputs may be any that keep to these rules, and one draw needn't show every extreme that they name: `expert_ids`: among the 8 tokens of one block no expert is named more than 3 times, and in some block some expert is named exactly 3 times; a token names 8 different experts.
All inputs are finite; a program needn't handle non-finite values.
Results may differ from a plain program's by a relative error of at most 0.028.
Values may be sent and summed in bfloat16 or wider, within the bound.
No kernel may reach another device: no remote copies, remote signals or barrier semaphores. Data moves between devices by JAX's collectives and lax.ppermute only.
A program may use at most 32 MiB of HBM per device.

v0:
```python
import jax
import jax.numpy as jnp
from jax import lax
from jax.sharding import PartitionSpec as P


def slot_table(id_block, experts, capacity):
    flat_ids = id_block.reshape(-1)
    onehot = (flat_ids[:, None] == jnp.arange(experts, dtype=jnp.int32)[None, :]).astype(jnp.int32)
    before = jnp.cumsum(onehot, axis=0) - onehot
    slot_index = jnp.sum(before * onehot, axis=1)
    target = flat_ids * capacity + slot_index
    row_index = jnp.arange(experts * capacity, dtype=jnp.int32)
    return (row_index[:, None] == target[None, :]).astype(jnp.bfloat16)


def gate_grads(hidden_grad, gate, up_value):
    sigmoid_gate = jax.nn.sigmoid(gate)
    silu_gate = gate * sigmoid_gate
    gate_grad = (
        hidden_grad * up_value * sigmoid_gate * (1.0 + gate * (1.0 - sigmoid_gate))
    ).astype(jnp.bfloat16)
    up_grad = (hidden_grad * silu_gate).astype(jnp.bfloat16)
    return (gate_grad, up_grad)


def contract_rows(left, right):
    return lax.dot_general(
        left, right, (((0,), (0,)), ((), ())), preferred_element_type=jnp.float32
    )


def contract_cols(left, right):
    return lax.dot_general(
        left, right, (((1,), (1,)), ((), ())), preferred_element_type=jnp.float32
    )


def local(tokens, expert_ids, route_weights, w_gate, w_up, w_down, grad_out):
    tok_rows = tokens.shape[0]
    slices = tokens.shape[1]
    top_count = expert_ids.shape[1]
    experts = lax.axis_size("expert")
    capacity = min(tok_rows, 3 * tok_rows * top_count // experts)
    table = slot_table(expert_ids, experts, capacity)
    weight_flat = route_weights.reshape(-1)
    token_replicas = jnp.repeat(tokens, top_count, axis=0)
    grad_rep = (
        jnp.repeat(grad_out, top_count, axis=0).astype(jnp.float32) * weight_flat[:, None]
    ).astype(jnp.bfloat16)
    dispatch_token_rows = jnp.dot(table, token_replicas, preferred_element_type=jnp.float32).astype(
        jnp.bfloat16
    )
    dispatch_gradients = jnp.dot(table, grad_rep, preferred_element_type=jnp.float32).astype(
        jnp.bfloat16
    )
    dispatch_token_rows = dispatch_token_rows.reshape(experts, capacity, slices)
    dispatch_gradients = dispatch_gradients.reshape(experts, capacity, slices)
    expert_in, expert_grad = (
        lax.all_to_all(dispatch_token_rows, "expert", split_axis=0, concat_axis=0, tiled=True),
        lax.all_to_all(dispatch_gradients, "expert", split_axis=0, concat_axis=0, tiled=True),
    )
    expert_in = expert_in.reshape(-1, slices)
    expert_grad = expert_grad.reshape(-1, slices)
    gate_matrix = w_gate[0]
    up_matrix = w_up[0]
    down_matrix = w_down[0]
    gate_part = jnp.dot(expert_in, gate_matrix, preferred_element_type=jnp.float32)
    up_part = jnp.dot(expert_in, up_matrix, preferred_element_type=jnp.float32)
    gate_piece, up_piece = (
        lax.psum_scatter(
            gate_part.astype(jnp.bfloat16), "dp", scatter_dimension=1, tiled=True
        ).astype(jnp.float32),
        lax.psum_scatter(
            up_part.astype(jnp.bfloat16), "dp", scatter_dimension=1, tiled=True
        ).astype(jnp.float32),
    )
    hidden_piece = (gate_piece * jax.nn.sigmoid(gate_piece) * up_piece).astype(jnp.bfloat16)
    hidden = lax.all_gather(hidden_piece, "dp", axis=1, tiled=True)
    expert_out = jnp.dot(hidden, down_matrix, preferred_element_type=jnp.float32).astype(
        jnp.bfloat16
    )
    out_blocks = expert_out.reshape(experts, capacity, slices)
    grad_part = contract_cols(expert_grad, down_matrix)
    grad_piece = lax.psum_scatter(
        grad_part.astype(jnp.bfloat16), "dp", scatter_dimension=1, tiled=True
    ).astype(jnp.float32)
    gate_grad_piece, up_grad_piece = gate_grads(grad_piece, gate_piece, up_piece)
    gate_grad, up_grad = (
        lax.all_gather(gate_grad_piece, "dp", axis=1, tiled=True),
        lax.all_gather(up_grad_piece, "dp", axis=1, tiled=True),
    )
    down_grad = contract_rows(hidden, expert_grad).astype(jnp.bfloat16)
    gate_weight = contract_rows(expert_in, gate_grad).astype(jnp.bfloat16)
    up_weight = contract_rows(expert_in, up_grad).astype(jnp.bfloat16)
    input_rows = (contract_cols(gate_grad, gate_matrix) + contract_cols(up_grad, up_matrix)).astype(
        jnp.bfloat16
    )
    input_blocks = input_rows.reshape(experts, capacity, slices)
    out_back, input_back = (
        lax.all_to_all(out_blocks, "expert", split_axis=0, concat_axis=0, tiled=True),
        lax.all_to_all(input_blocks, "expert", split_axis=0, concat_axis=0, tiled=True),
    )
    backward_output = contract_rows(table, out_back.reshape(-1, slices)).reshape(
        tok_rows, top_count, slices
    )
    backward_input = contract_rows(table, input_back.reshape(-1, slices)).reshape(
        tok_rows, top_count, slices
    )
    layer_out = jnp.sum(backward_output * route_weights[:, :, None], axis=1).astype(jnp.bfloat16)
    input_grad = jnp.sum(backward_input, axis=1).astype(jnp.bfloat16)
    return (layer_out, input_grad, gate_weight[None], up_weight[None], down_grad[None])


def solution(mesh):
    return jax.shard_map(
        local,
        mesh=mesh,
        in_specs=(
            P("expert", "dp"),
            P("expert", None),
            P("expert", None),
            P("expert", "dp", None),
            P("expert", "dp", None),
            P("expert", None, "dp"),
            P("expert", "dp"),
        ),
        out_specs=(
            P("expert", "dp"),
            P("expert", "dp"),
            P("expert", "dp", None),
            P("expert", "dp", None),
            P("expert", None, "dp"),
        ),
        check_vma=False,
    )
```

profile of v0, /device:TPU:8, one launch (start us, length us, event | category | flops | bytes accessed | tf_op | source)
XLA Modules:
  0.0 350.0 jit_solution(8880993989482910825)
XLA Ops:
  7.2 0.0 reduce-scatter.4.cloned.1.call-start
  7.2 0.8 reshape.93
  8.0 0.1 fusion.33
  8.1 0.1 reduce_window_sum.11
  8.2 0.2 select_reduce_fusion
  8.4 0.5 copy-done.3
  8.9 0.2 convolution_convert_fusion.8
  9.1 0.1 reshape.95
  9.1 39.7 %all_to_all.20 = bf16[64,3,256]{2,1,0:T(4,128)(2,1)S(1)} all-to-all(bf16[64,3,256]{2,1,0:T(4,128)(2,1)S(1)} %reshape.95), channel_id=1, replica_groups=mesh['dp'=16,'expert'=64] {'expert'}, dimensions={0} | all-to-all | bytes 196608 | tf_op jit(solution)/shard_map/all_to_all | solution.py:60
  48.8 0.1 reshape.96
  48.9 1.1 convolution_convert_fusion.5
  50.0 0.0 reduce-scatter.4.cloned.1.call-update
  50.0 0.7 copy-done.4
  50.7 0.0 copy-done.5
  50.7 0.1 mul.60
  50.8 0.2 convolution_convert_fusion.6
  51.0 0.7 reshape.99
  51.7 4.6 %all-to-all-start.2 = ((bf16[64,3,256]{2,1,0:T(4,128)(2,1)}), bf16[64,3,256]{2,1,0:T(4,128)(2,1)S(1)}, u32[]{:S(2)}, u32[]{:S(2)}) async-start(bf16[64,3,256]{2,1,0:T(4,128)(2,1)} %reshape.99), calls=%async_computation.4 | async-start | bytes 262144 | tf_op jit(solution)/shard_map/all_to_all | solution.py:61
  56.3 0.0 reduce-scatter.6.cloned.1.call-start
  56.4 1.1 convolution_convert_fusion.4
  57.5 0.0 reduce-scatter.6.cloned.1.call-update
  57.5 0.0 reduce-scatter.8.cloned.1.call-start
  57.5 15.6 %all-to-all-done.2 = bf16[64,3,256]{2,1,0:T(4,128)(2,1)S(1)} async-done(((bf16[64,3,256]{2,1,0:T(4,128)(2,1)}), bf16[64,3,256]{2,1,0:T(4,128)(2,1)S(1)}, u32[]{:S(2)}, u32[]{:S(2)}) %all-to-all-start.2) | async-done | bytes 98336 | tf_op jit(solution)/shard_map/all_to_all | solution.py:61
  73.1 0.1 reshape.100
  73.2 1.0 convolution_convert_fusion.3
  74.3 0.0 reduce-scatter.8.cloned.1.call-update
  74.3 27.9 %reduce-scatter.4.cloned.1.call-done = bf16[192,48]{0,1:T(8,128)(2,1)} async-done(((bf16[192,768]{0,1:T(8,128)(2,1)}), bf16[192,48]{0,1:T(8,128)(2,1)}) %reduce-scatter.4.cloned.1.call-update) | async-done | bytes 18448 | tf_op jit(solution)/shard_map/reduce_scatter | solution.py:71
  102.2 67.7 %reduce-scatter.6.cloned.1.call-done = bf16[192,48]{0,1:T(8,128)(2,1)} async-done(((bf16[192,768]{0,1:T(8,128)(2,1)}), bf16[192,48]{0,1:T(8,128)(2,1)}) %reduce-scatter.6.cloned.1.call-update) | async-done | bytes 18448 | tf_op jit(solution)/shard_map/reduce_scatter | solution.py:74
  169.9 68.1 %reduce-scatter.8.cloned.1.call-done = bf16[192,48]{0,1:T(8,128)(2,1)} async-done(((bf16[192,768]{0,1:T(8,128)(2,1)}), bf16[192,48]{0,1:T(8,128)(2,1)}) %reduce-scatter.8.cloned.1.call-update) | async-done | bytes 18448 | tf_op jit(solution)/shard_map/reduce_scatter | solution.py:85
  237.9 0.8 fusion.20
  238.8 18.7 %all_gather.10 = bf16[192,768]{0,1:T(8,128)(2,1)S(1)} all-gather(bf16[192,48]{0,1:T(8,128)(2,1)S(1)} %get-tuple-element.6), channel_id=1, replica_groups=mesh['dp'=16,'expert'=64] {'dp'}, dimensions={1}, use_global_device_ids=true | all-gather | bytes 313344 | tf_op jit(solution)/shard_map/all_gather | solution.py:90
  257.4 0.3 fusion.9
  257.7 15.2 %all_gather.11 = bf16[192,768]{0,1:T(8,128)(2,1)S(1)} all-gather(bf16[192,48]{0,1:T(8,128)(2,1)S(1)} %get-tuple-element.5), channel_id=1, replica_groups=mesh['dp'=16,'expert'=64] {'dp'}, dimensions={1}, use_global_device_ids=true | all-gather | bytes 313344 | tf_op jit(solution)/shard_map/all_gather | solution.py:91
  273.0 0.3 fusion.3
  273.3 0.7 reshape.101
  274.0 16.2 %all-to-all-start.3 = ((bf16[64,3,256]{2,1,0:T(4,128)(2,1)}), bf16[64,3,256]{2,1,0:T(4,128)(2,1)S(1)}, u32[]{:S(2)}, u32[]{:S(2)}) async-start(bf16[64,3,256]{2,1,0:T(4,128)(2,1)} %reshape.101), calls=%async_computation.6 | async-start | bytes 262144 | tf_op jit(solution)/shard_map/all_to_all | solution.py:102
  290.2 17.1 %all_gather.9 = bf16[192,768]{0,1:T(8,128)(2,1)S(1)} all-gather(bf16[192,48]{0,1:T(8,128)(2,1)S(1)} %get-tuple-element.7), channel_id=1, replica_groups=mesh['dp'=16,'expert'=64] {'dp'}, dimensions={1}, use_global_device_ids=true | all-gather | bytes 313344 | tf_op jit(solution)/shard_map/all_gather | solution.py:79
  307.3 0.3 convolution_convert_fusion.7
  307.6 0.7 reshape.97
  308.3 1.1 fusion
  309.4 15.1 %all-to-all-start.1 = ((bf16[64,3,256]{2,1,0:T(4,128)(2,1)}), bf16[64,3,256]{2,1,0:T(4,128)(2,1)S(1)}, u32[]{:S(2)}, u32[]{:S(2)}) async-start(bf16[64,3,256]{2,1,0:T(4,128)(2,1)} %reshape.97), calls=%async_computation.3 | async-start | bytes 262144 | tf_op jit(solution)/shard_map/all_to_all | solution.py:101
  324.5 1.1 fusion.1
  325.5 1.0 fusion.2
  326.5 0.1 reshape.104
  326.6 0.8 convolution_reduce_fusion
  327.4 15.2 %all-to-all-done.1 = bf16[64,3,256]{2,1,0:T(4,128)(2,1)S(1)} async-done(((bf16[64,3,256]{2,1,0:T(4,128)(2,1)}), bf16[64,3,256]{2,1,0:T(4,128)(2,1)S(1)}, u32[]{:S(2)}, u32[]{:S(2)}) %all-to-all-start.1) | async-done | bytes 98336 | tf_op jit(solution)/shard_map/all_to_all | solution.py:101
  342.6 0.1 reshape.103
  342.7 0.8 fusion.4
  (12 shorter events, 0.0 us)
Async XLA Ops:
  7.2 41.8 %copy-start = (bf16[1,256,768]{2,1,0:T(8,128)(2,1)S(1)}, bf16[1,256,768]{2,1,0:T(8,128)(2,1)}, u32[]{:S(2)}) copy-start(bf16[1,256,768]{2,1,0:T(8,128)(2,1)} %param.10) | copy-start | bytes 1179652
  7.2 95.0 %reduce-scatter.4.cloned.1.call-start = ((), (), s32[]{:S(2)}) async-start(), calls=%async_computation.7 | async-start | bytes 417792 | tf_op jit(solution)/shard_map/reduce_scatter | solution.py:71
  8.2 0.7 copy-start.3
  50.0 0.7 copy-start.4
  50.0 0.7 copy-start.5
  50.7 5.7 %copy-start.1 = (bf16[1,256,768]{2,1,0:T(8,128)(2,1)S(1)}, bf16[1,256,768]{2,1,0:T(8,128)(2,1)}, u32[]{:S(2)}) copy-start(bf16[1,256,768]{2,1,0:T(8,128)(2,1)} %param.11) | copy-start | bytes 1179652
  51.7 21.4 %all-to-all-start.2 = ((bf16[64,3,256]{2,1,0:T(4,128)(2,1)}), bf16[64,3,256]{2,1,0:T(4,128)(2,1)S(1)}, u32[]{:S(2)}, u32[]{:S(2)}) async-start(bf16[64,3,256]{2,1,0:T(4,128)(2,1)} %reshape.99), calls=%async_computation.4 | async-start | bytes 262144 | tf_op jit(solution)/shard_map/all_to_all | solution.py:61
  56.3 113.5 %reduce-scatter.6.cloned.1.call-start = ((), (), s32[]{:S(2)}) async-start(), calls=%async_computation.8 | async-start | bytes 417792 | tf_op jit(solution)/shard_map/reduce_scatter | solution.py:74
  57.5 15.8 %copy-start.2 = (bf16[1,768,256]{2,1,0:T(8,128)(2,1)S(1)}, bf16[1,768,256]{2,1,0:T(8,128)(2,1)}, u32[]{:S(2)}) copy-start(bf16[1,768,256]{2,1,0:T(8,128)(2,1)} %param.12) | copy-start | bytes 1179652
  57.5 180.4 %reduce-scatter.8.cloned.1.call-start = ((), (), s32[]{:S(2)}) async-start(), calls=%async_computation.9 | async-start | bytes 417792 | tf_op jit(solution)/shard_map/reduce_scatter | solution.py:85
  274.0 35.4 %all-to-all-start.3 = ((bf16[64,3,256]{2,1,0:T(4,128)(2,1)}), bf16[64,3,256]{2,1,0:T(4,128)(2,1)S(1)}, u32[]{:S(2)}, u32[]{:S(2)}) async-start(bf16[64,3,256]{2,1,0:T(4,128)(2,1)} %reshape.101), calls=%async_computation.6 | async-start | bytes 262144 | tf_op jit(solution)/shard_map/all_to_all | solution.py:102
  309.4 33.2 %all-to-all-start.1 = ((bf16[64,3,256]{2,1,0:T(4,128)(2,1)}), bf16[64,3,256]{2,1,0:T(4,128)(2,1)S(1)}, u32[]{:S(2)}, u32[]{:S(2)}) async-start(bf16[64,3,256]{2,1,0:T(4,128)(2,1)} %reshape.97), calls=%async_computation.3 | async-start | bytes 262144 | tf_op jit(solution)/shard_map/all_to_all | solution.py:101
Sparse Core Ops, SparseCore 0:
  50.1 51.9 reduce-scatter.3
  106.1 63.7 reduce-scatter.5
  173.8 64.0 reduce-scatter.7
where the time goes:
time: 351 us; the launch traced here: 350 us
  waiting for transfers between devices  194 us (55%)
  blocking collectives  90.7 us (26%)
  starting transfers between devices  36 us (10%)
  between operations  13.9 us (4%)
  matrix products  9.18 us (3%)
  local copies, waits for them, and re-layouts  4.58 us (1%)
    reduce_scatter x1, waiting for transfers between devices, local(): lax.psum_scatter(grad_part.astype(jnp.bfloat16), 'dp', scatter_dimension=...  68.1 us
    reduce_scatter x1, waiting for transfers between devices, local(): lax.psum_scatter(up_part.astype(jnp.bfloat16), 'dp', scatter_dimension=1,...  67.7 us
    all_to_all x1, blocking collectives, local(): lax.all_to_all(dispatch_token_rows, 'expert', split_axis=0, concat_axis=0...  39.7 us
    reduce_scatter x1, waiting for transfers between devices, local(): lax.psum_scatter(gate_part.astype(jnp.bfloat16), 'dp', scatter_dimension=...  27.9 us
    all_gather x1, blocking collectives, local(): lax.all_gather(gate_grad_piece, 'dp', axis=1, tiled=True)  18.7 us
    all_gather x1, blocking collectives, local(): hidden = lax.all_gather(hidden_piece, 'dp', axis=1, tiled=True)  17.1 us
    all_to_all x1, starting transfers between devices, local(): lax.all_to_all(input_blocks, 'expert', split_axis=0, concat_axis=0, tiled...  16.2 us
    all_to_all x1, waiting for transfers between devices, local(): lax.all_to_all(dispatch_gradients, 'expert', split_axis=0, concat_axis=0,...  15.6 us
  transfers between devices with their start and end apart: 6, of which 5 were waited for; matrix products, arithmetic and copies ran while one was open for 2% of the time, Pallas kernels for 0%

commit v1 on v0

v1 whole, which is shorter than its diff:
```python
import jax
import jax.numpy as jnp
from jax import lax
from jax.sharding import PartitionSpec as P

BF = jnp.bfloat16
F32 = jnp.float32


def slot_table(id_block, experts, capacity):
    flat_ids = id_block.reshape(-1)
    onehot = (flat_ids[:, None] == jnp.arange(experts, dtype=jnp.int32)[None, :]).astype(jnp.int32)
    before = jnp.cumsum(onehot, axis=0) - onehot
    slot_index = jnp.sum(before * onehot, axis=1)
    target = flat_ids * capacity + slot_index
    row_index = jnp.arange(experts * capacity, dtype=jnp.int32)
    return (row_index[:, None] == target[None, :]).astype(BF)


def gate_grads(hidden_grad, gate, up_value):
    sigmoid_gate = jax.nn.sigmoid(gate)
    silu_gate = gate * sigmoid_gate
    gate_grad = (
        hidden_grad * up_value * sigmoid_gate * (1.0 + gate * (1.0 - sigmoid_gate))
    ).astype(BF)
    up_grad = (hidden_grad * silu_gate).astype(BF)
    return (gate_grad, up_grad)


def mm(left, right, lc, rc):
    return lax.dot_general(left, right, (((lc,), (rc,)), ((), ())), preferred_element_type=F32)


def local(tokens, expert_ids, route_weights, w_gate, w_up, w_down, grad_out):
    tok_rows, slices = tokens.shape
    top_count = expert_ids.shape[1]
    experts = lax.axis_size("expert")
    dp = lax.axis_size("dp")
    capacity = min(tok_rows, 3 * tok_rows * top_count // experts)
    rows = experts * capacity
    gate_matrix, up_matrix, down_matrix = w_gate[0], w_up[0], w_down[0]
    ff = gate_matrix.shape[1]
    half = ff // 2
    chips = dp // 2
    group = rows // chips
    lanes = 2 * slices // 128

    table = slot_table(expert_ids, experts, capacity)
    weight_flat = route_weights.reshape(-1)
    token_rep = jnp.repeat(tokens, top_count, axis=0)
    grad_rep = (
        jnp.repeat(grad_out, top_count, axis=0).astype(F32) * weight_flat[:, None]
    ).astype(BF)
    packed = mm(table, jnp.concatenate([token_rep, grad_rep], axis=1), 1, 0).astype(BF)
    received = lax.all_to_all(
        packed.reshape(experts, capacity, lanes, 128), "expert", split_axis=0, concat_axis=0, tiled=True
    ).reshape(rows, 2 * slices)
    expert_in, expert_grad = received[:, :slices], received[:, slices:]

    gate_part = mm(expert_in, gate_matrix, 1, 0).astype(BF)
    up_part = mm(expert_in, up_matrix, 1, 0).astype(BF)
    grad_part = mm(expert_grad, down_matrix, 1, 1).astype(BF)

    def halves(c):
        cut = slice(c * half, (c + 1) * half)
        return jnp.concatenate([gate_part[:, cut], up_part[:, cut], grad_part[:, cut]], axis=1)

    stacked = jnp.stack([halves(0).reshape(chips, group, 3 * half), halves(1).reshape(chips, group, 3 * half)], axis=1)
    parts = lax.all_to_all(
        stacked.reshape(dp, group, 3 * half), "dp", split_axis=0, concat_axis=0, tiled=True
    )
    sums = jnp.sum(parts.astype(F32), axis=0)
    gate, up, hidden_grad = sums[:, :half], sums[:, half : 2 * half], sums[:, 2 * half :]
    hidden_piece = (gate * jax.nn.sigmoid(gate) * up).astype(BF)
    gate_grad_piece, up_grad_piece = gate_grads(hidden_grad, gate, up)
    pieces = jnp.concatenate([hidden_piece, gate_grad_piece, up_grad_piece], axis=1)

    gathered = lax.all_gather(pieces, "dp", axis=0, tiled=True).reshape(chips, 2, group, 3 * half)
    cols = [gathered[:, c].reshape(rows, 3 * half) for c in range(2)]
    hidden, gate_grad, up_grad = (
        jnp.concatenate([cols[c][:, i * half : (i + 1) * half] for c in range(2)], axis=1) for i in range(3)
    )

    expert_out = mm(hidden, down_matrix, 1, 0).astype(BF)
    input_rows = (mm(gate_grad, gate_matrix, 1, 1) + mm(up_grad, up_matrix, 1, 1)).astype(BF)
    back = lax.all_to_all(
        jnp.concatenate([expert_out, input_rows], axis=1).reshape(experts, capacity, lanes, 128),
        "expert", split_axis=0, concat_axis=0, tiled=True,
    ).reshape(rows, 2 * slices)

    down_grad = mm(hidden, expert_grad, 0, 0).astype(BF)
    gate_weight = mm(expert_in, gate_grad, 0, 0).astype(BF)
    up_weight = mm(expert_in, up_grad, 0, 0).astype(BF)

    choice = mm(table, back, 0, 0).reshape(tok_rows, top_count, 2 * slices)
    layer_out = jnp.sum(choice[:, :, :slices] * route_weights[:, :, None], axis=1).astype(BF)
    input_grad = jnp.sum(choice[:, :, slices:], axis=1).astype(BF)
    return (layer_out, input_grad, gate_weight[None], up_weight[None], down_grad[None])


def solution(mesh):
    return jax.shard_map(
        local,
        mesh=mesh,
        in_specs=(
            P("expert", "dp"),
            P("expert", None),
            P("expert", None),
            P("expert", "dp", None),
            P("expert", "dp", None),
            P("expert", None, "dp"),
            P("expert", "dp"),
        ),
        out_specs=(
            P("expert", "dp"),
            P("expert", "dp"),
            P("expert", "dp", None),
            P("expert", "dp", None),
            P("expert", None, "dp"),
        ),
        check_vma=False,
    )
```

time: 351 us -> 126 us (0.36)
  waiting for transfers between devices: 194 us -> 17.9 us
  starting transfers between devices: 36 us -> 4.61 us
  between operations: 13.9 us -> 0.84 us
  matrix products: 9.18 us -> 5.17 us
    reduce_scatter x3 -> x0, waiting for transfers between devices: 164 us -> none  [the longest x1 68.1 us: local(): lax.psum_scatter(grad_part.astype(jnp.bfloat16), 'dp', scatter_dimension=...]
    all_gather x3 -> x1, blocking collectives: 51 us -> 18.5 us  [local(): lax.all_gather(pieces, 'dp', axis=0, tiled=True)]
    all_to_all x1 -> x2, blocking collectives: 39.7 us -> 72.2 us  [the longest x1 42.2 us: local(): lax.all_to_all(packed.reshape(experts, capacity, lanes, 128), 'expert', s...]
    all_to_all x3 -> x1, starting transfers between devices: 35.9 us -> 4.61 us  [local(): lax.all_to_all(jnp.concatenate([expert_out, input_rows], axis=1).reshape(...]
    all_to_all x3 -> x1, waiting for transfers between devices: 30.7 us -> 17.9 us  [local(): lax.all_to_all(jnp.concatenate([expert_out, input_rows], axis=1).reshape(...]
    dot_general x13 -> x11, matrix products: 9.18 us -> 5.17 us  [mm(): lax.dot_general(left, right, (((lc,), (rc,)), ((), ())), preferred_elemen...]
  transfers between devices with their start and end apart: 6 -> 1, of which waited for: 5 -> 1; matrix products, arithmetic and copies ran while one was open for 2% -> 3% of each run, Pallas kernels for 0% -> 0%
where the time goes in v1:
time: 126 us; the launch traced here: 125 us
  blocking collectives  90.7 us (72%)
  waiting for transfers between devices  17.9 us (14%)
  matrix products  5.17 us (4%)
  starting transfers between devices  4.61 us (4%)
  local copies, waits for them, and re-layouts  4.06 us (3%)
  other arithmetic  2.16 us (2%)
    all_to_all x1, blocking collectives, local(): lax.all_to_all(packed.reshape(experts, capacity, lanes, 128), 'expert', s...  42.2 us
    all_to_all x1, blocking collectives, local(): lax.all_to_all(stacked.reshape(dp, group, 3 * half), 'dp', split_axis=0,...  30 us
    all_gather x1, blocking collectives, local(): lax.all_gather(pieces, 'dp', axis=0, tiled=True)  18.5 us
    all_to_all x1, waiting for transfers between devices, local(): lax.all_to_all(jnp.concatenate([expert_out, input_rows], axis=1).reshape(...  17.9 us
    dot_general x11, matrix products, mm(): lax.dot_general(left, right, (((lc,), (rc,)), ((), ())), preferred_elemen...  5.17 us
    all_to_all x1, starting transfers between devices, local(): lax.all_to_all(jnp.concatenate([expert_out, input_rows], axis=1).reshape(...  4.61 us
  transfers between devices with their start and end apart: 1, of which 1 were waited for; matrix products, arithmetic and copies ran while one was open for 3% of the time, Pallas kernels for 0%

profile of v1, /device:TPU:8, one launch (start us, length us, event | category | flops | bytes accessed | tf_op | source)
XLA Modules:
  0.0 125.4 jit_solution(18254271364089752921)
XLA Ops:
  0.6 0.0 copy-start
  0.6 0.0 copy-start.1
  0.7 0.8 reshape.73
  1.5 0.8 mul.56
  2.3 0.7 convert_element_type.60
  3.0 0.1 fusion.28
  3.0 0.1 reduce_window_sum.11
  3.1 0.2 select_reduce_fusion
  3.3 0.7 broadcast_bitcast_fusion
  4.0 0.1 fusion.17
  4.1 0.2 convolution_convert_fusion.6
  4.3 0.1 reshape.75
  4.3 42.2 %all_to_all.15 = bf16[64,3,4,128]{3,2,1,0:T(4,128)(2,1)S(1)} all-to-all(bf16[64,3,4,128]{3,2,1,0:T(4,128)(2,1)S(1)} %reshape.75), channel_id=1, replica_groups=mesh['dp'=16,'expert'=64] {'expert'}, dimensions={0} | all-to-all | bytes 393216 | tf_op jit(solution)/shard_map/all_to_all | solution.py:55
  46.6 0.0 copy-done.1
  46.6 0.2 convolution_convert_fusion.4
  46.9 0.0 copy-start.2
  46.9 0.0 copy-done
  46.9 0.3 convolution_convert_fusion.3
  47.3 0.6 copy-done.2
  47.9 0.2 convolution_convert_fusion.5
  48.2 0.1 pad_maximum_fusion.1
  48.3 0.1 pad_maximum_fusion
  48.4 30.0 %all_to_all.16 = bf16[16,24,1152]{2,1,0:T(8,128)(2,1)S(1)} all-to-all(bf16[16,24,1152]{2,1,0:T(8,128)(2,1)S(1)} %bitcast.47), channel_id=1, replica_groups=mesh['dp'=16,'expert'=64] {'dp'}, dimensions={0} | all-to-all | bytes 1769472 | tf_op jit(solution)/shard_map/all_to_all | solution.py:69
  78.4 0.1 convert_reduce_fusion
  78.5 18.5 %all_gather.3 = bf16[384,1152]{1,0:T(8,128)(2,1)S(1)} all-gather(bf16[24,1152]{1,0:T(8,128)(2,1)S(1)} %pad_maximum_fusion.13), channel_id=1, replica_groups=mesh['dp'=16,'expert'=64] {'dp'}, dimensions={0}, use_global_device_ids=true | all-gather | bytes 940032 | tf_op jit(solution)/shard_map/all_gather | solution.py:78
  97.0 0.1 fusion.36
  97.2 0.2 convolution_convert_fusion.7
  97.4 0.3 fusion.8
  97.7 0.3 fusion.3
  98.1 0.7 reshape.79
  98.8 4.6 %all-to-all-start.2 = ((bf16[64,3,4,128]{3,2,1,0:T(4,128)(2,1)}), bf16[64,3,4,128]{3,2,1,0:T(4,128)(2,1)S(1)}, u32[]{:S(2)}, u32[]{:S(2)}) async-start(bf16[64,3,4,128]{3,2,1,0:T(4,128)(2,1)} %reshape.79), calls=%async_computation.2 | async-start | bytes 393216 | tf_op jit(solution)/shard_map/all_to_all | solution.py:86
  103.4 1.0 fusion.1
  104.4 1.0 fusion
  105.5 0.0 copy-start.3
  105.5 1.1 fusion.2
  106.5 17.9 %all-to-all-done.2 = bf16[64,3,4,128]{3,2,1,0:T(4,128)(2,1)S(1)} async-done(((bf16[64,3,4,128]{3,2,1,0:T(4,128)(2,1)}), bf16[64,3,4,128]{3,2,1,0:T(4,128)(2,1)S(1)}, u32[]{:S(2)}, u32[]{:S(2)}) %all-to-all-start.2) | async-done | bytes 196640 | tf_op jit(solution)/shard_map/all_to_all | solution.py:86
  124.4 0.1 reshape.81
  124.5 0.2 fusion.19
  124.7 0.0 copy-done.3
  124.7 0.7 slice_reduce_fusion
  (10 shorter events, 0.3 us)
Async XLA Ops:
  0.6 46.3 %copy-start = (bf16[1,768,256]{2,1,0:T(8,128)(2,1)S(1)}, bf16[1,768,256]{2,1,0:T(8,128)(2,1)}, u32[]{:S(2)}) copy-start(bf16[1,768,256]{2,1,0:T(8,128)(2,1)} %param.12) | copy-start | bytes 1179652
  0.6 46.0 %copy-start.1 = (bf16[1,256,768]{2,1,0:T(8,128)(2,1)S(1)}, bf16[1,256,768]{2,1,0:T(8,128)(2,1)}, u32[]{:S(2)}) copy-start(bf16[1,256,768]{2,1,0:T(8,128)(2,1)} %param.11) | copy-start | bytes 1179652
  46.9 1.0 copy-start.2
  98.8 25.6 %all-to-all-start.2 = ((bf16[64,3,4,128]{3,2,1,0:T(4,128)(2,1)}), bf16[64,3,4,128]{3,2,1,0:T(4,128)(2,1)S(1)}, u32[]{:S(2)}, u32[]{:S(2)}) async-start(bf16[64,3,4,128]{3,2,1,0:T(4,128)(2,1)} %reshape.79), calls=%async_computation.2 | async-start | bytes 393216 | tf_op jit(solution)/shard_map/all_to_all | solution.py:86
  105.5 19.2 %copy-start.3 = (f32[8,8]{1,0:T(8,128)S(1)}, f32[8,8]{1,0:T(8,128)}, u32[]{:S(2)}) copy-start(f32[8,8]{1,0:T(8,128)} %param.9) | copy-start | bytes 772

commit v2 on v1

v2 whole, which is shorter than its diff:
```python
import jax
import jax.numpy as jnp
from jax import lax
from jax.experimental import pallas as pl
from jax.experimental.pallas import tpu as pltpu
from jax.sharding import PartitionSpec as P

BF = jnp.bfloat16
F32 = jnp.float32
VMEM = pl.BlockSpec(memory_space=pltpu.VMEM)


def dot(left, right, lc, rc, precision=None):
    return lax.dot_general(
        left, right, (((lc,), (rc,)), ((), ())), preferred_element_type=F32, precision=precision
    )


def dispatch_body(capacity, ids_ref, weights_ref, tokens_ref, grads_ref, rows_ref, pick_ref, scaled_ref):
    tok, top = ids_ref.shape
    rows = rows_ref.shape[0]
    experts = rows // capacity
    width = tokens_ref.shape[1]
    ids, weights = ids_ref[...], weights_ref[...]
    expert = lax.broadcasted_iota(jnp.int32, (tok, experts), 1)
    named = jnp.zeros((tok, experts), F32)
    weight = jnp.zeros((tok, experts), F32)
    for k in range(top):
        hit = ids[:, k : k + 1] == expert
        named = named + jnp.where(hit, 1.0, 0.0)
        weight = weight + jnp.where(hit, weights[:, k : k + 1], 0.0)
    earlier = lax.broadcasted_iota(jnp.int32, (tok, tok), 0) > lax.broadcasted_iota(jnp.int32, (tok, tok), 1)
    slot = dot(jnp.where(earlier, 1.0, 0.0), named, 1, 0)
    row = lax.broadcasted_iota(jnp.int32, (rows, experts), 0)
    owner = lax.broadcasted_iota(jnp.int32, (rows, experts), 1)
    first = owner * capacity
    spread = jnp.where((row >= first) & (row < first + capacity), 1.0, 0.0)
    row_id = lax.broadcasted_iota(jnp.int32, (rows, tok), 0)
    row_slot = lax.rem(row_id, capacity).astype(F32)
    chosen = dot(spread, jnp.where(named > 0.5, slot, -1.0), 1, 1)
    pick = jnp.where(jnp.abs(chosen - row_slot) < 0.5, 1.0, 0.0)
    row_weight = dot(spread, weight, 1, 1, lax.Precision.HIGHEST)
    scale = jnp.sum(pick * row_weight, axis=1, keepdims=True)
    rows_ref[:, :width] = dot(pick, tokens_ref[...].astype(F32), 1, 0).astype(BF)
    rows_ref[:, width:] = (dot(pick, grads_ref[...].astype(F32), 1, 0) * scale).astype(BF)
    pick_ref[...] = pick
    scaled_ref[...] = pick * scale


def dispatch(ids, weights, tokens, grads, rows, capacity):
    tok, width = tokens.shape

    def body(*refs):
        dispatch_body(capacity, *refs)

    return pl.pallas_call(
        body,
        out_shape=(
            pltpu.VMEM((rows, 2 * width), BF),
            pltpu.VMEM((rows, tok), F32),
            pltpu.VMEM((rows, tok), F32),
        ),
        in_specs=[VMEM] * 4,
        out_specs=(VMEM,) * 3,
    )(ids, weights, tokens, grads)


def near(*arrays):
    return [pltpu.with_memory_space_constraint(x, pltpu.VMEM) for x in arrays]


def share(side, rows_ref, gate_ref, up_ref, down_ref):
    width = rows_ref.shape[1] // 2
    half = gate_ref.shape[2] // 2
    cut = pl.ds(pl.multiple_of(side * half, half), half)
    yield slice(0, half), dot(rows_ref[:, :width], gate_ref[0, :, cut], 1, 0)
    yield slice(half, 2 * half), dot(rows_ref[:, :width], up_ref[0, :, cut], 1, 0)
    yield slice(2 * half, 3 * half), dot(rows_ref[:, width:], down_ref[0, cut, :], 1, 1)


def theirs_body(rows_ref, gate_ref, up_ref, down_ref, theirs_ref):
    core = lax.rem(lax.axis_index("dp"), 2)
    for cols, value in share(1 - core, rows_ref, gate_ref, up_ref, down_ref):
        theirs_ref[:, cols] = value.astype(BF)


def theirs_share(received, matrices):
    return pl.pallas_call(
        theirs_body,
        out_shape=pltpu.VMEM((received.shape[0], 3 * matrices[0].shape[2] // 2), BF),
        in_specs=[VMEM] * 4,
        out_specs=VMEM,
    )(*near(received), *matrices)


def pair_body(both_ref, rows_ref, gate_ref, up_ref, down_ref, pair_ref):
    rows = rows_ref.shape[0]
    core = lax.rem(lax.axis_index("dp"), 2)
    other = pl.ds(pl.multiple_of((1 - core) * rows, rows), rows)
    for cols, value in share(core, rows_ref, gate_ref, up_ref, down_ref):
        pair_ref[:, cols] = (value + both_ref[other, cols].astype(F32)).astype(BF)


def pair_share(both, received, matrices):
    return pl.pallas_call(
        pair_body,
        out_shape=pltpu.VMEM((received.shape[0], both.shape[1]), BF),
        in_specs=[VMEM] * 5,
        out_specs=VMEM,
    )(*near(both, received), *matrices)


def finish_body(
    back_ref, pick_ref, scaled_ref, rows_ref, low_ref, high_ref, out_ref, in_ref, gate_ref, up_ref, down_ref,
    out_buf, in_buf, gate_buf, up_buf, down_buf, sems,
):
    width = rows_ref.shape[1] // 2
    half = low_ref.shape[1] // 3
    sides = (low_ref, high_ref)
    expert_in, expert_grad = rows_ref[:, :width], rows_ref[:, width:]
    stores = [
        pltpu.make_async_copy(buf, out, sems.at[i])
        for i, (buf, out) in enumerate(
            (
                (gate_buf, gate_ref.at[0]),
                (up_buf, up_ref.at[0]),
                (down_buf, down_ref.at[0]),
                (out_buf, out_ref),
                (in_buf, in_ref),
            )
        )
    ]
    for i, buf in enumerate((gate_buf, up_buf)):
        for c, side in enumerate(sides):
            grad = side[:, (i + 1) * half : (i + 2) * half]
            buf[:, c * half : (c + 1) * half] = dot(expert_in, grad, 0, 0).astype(BF)
        stores[i].start()
    for c, side in enumerate(sides):
        down_buf[c * half : (c + 1) * half, :] = dot(side[:, :half], expert_grad, 0, 0).astype(BF)
    stores[2].start()
    out_buf[...] = dot(scaled_ref[...], back_ref[:, :width].astype(F32), 0, 0, lax.Precision.HIGHEST).astype(BF)
    stores[3].start()
    in_buf[...] = dot(pick_ref[...], back_ref[:, width:].astype(F32), 0, 0).astype(BF)
    stores[4].start()
    for store in stores:
        store.wait()


def finish(back, pick, scaled, received, low, high):
    width, half = received.shape[1] // 2, low.shape[1] // 3
    tok = pick.shape[1]
    shapes = ((tok, width), (tok, width), (1, width, 2 * half), (1, width, 2 * half), (1, 2 * half, width))
    return pl.pallas_call(
        finish_body,
        out_shape=tuple(jax.ShapeDtypeStruct(s, BF) for s in shapes),
        in_specs=[VMEM] * 6,
        out_specs=(pl.BlockSpec(memory_space=pl.ANY),) * 5,
        scratch_shapes=[pltpu.VMEM(s[-2:], BF) for s in shapes] + [pltpu.SemaphoreType.DMA((5,))],
    )(*near(back, pick, scaled, received, low, high))


def back_body(low_ref, high_ref, gate_ref, up_ref, down_ref, rows_ref):
    width = rows_ref.shape[1] // 2
    half = low_ref.shape[1] // 3
    out, back = None, None
    for c, side in enumerate((low_ref, high_ref)):
        cut = slice(c * half, (c + 1) * half)
        one = dot(side[:, :half], down_ref[0, cut, :], 1, 0)
        two = dot(side[:, half : 2 * half], gate_ref[0, :, cut], 1, 1)
        two = two + dot(side[:, 2 * half :], up_ref[0, :, cut], 1, 1)
        out, back = (one, two) if c == 0 else (out + one, back + two)
    rows_ref[:, :width] = out.astype(BF)
    rows_ref[:, width:] = back.astype(BF)


def back_rows(low, high, matrices):
    return pl.pallas_call(
        back_body,
        out_shape=pltpu.VMEM((low.shape[0], 2 * matrices[0].shape[1]), BF),
        in_specs=[VMEM] * 5,
        out_specs=VMEM,
    )(*near(low, high), *matrices)


def gate_grads(hidden_grad, gate, up_value):
    sigmoid_gate = jax.nn.sigmoid(gate)
    silu_gate = gate * sigmoid_gate
    gate_grad = (
        hidden_grad * up_value * sigmoid_gate * (1.0 + gate * (1.0 - sigmoid_gate))
    ).astype(BF)
    up_grad = (hidden_grad * silu_gate).astype(BF)
    return (gate_grad, up_grad)


def local(tokens, expert_ids, route_weights, w_gate, w_up, w_down, grad_out):
    tok_rows, slices = tokens.shape
    top_count = expert_ids.shape[1]
    experts = lax.axis_size("expert")
    dp = lax.axis_size("dp")
    capacity = min(tok_rows, 3 * tok_rows * top_count // experts)
    rows = experts * capacity
    half = w_gate.shape[2] // 2
    chips = dp // 2
    group = rows // chips
    lanes = 2 * slices // 128

    packed, pick, scaled = dispatch(expert_ids, route_weights, tokens, grad_out, rows, capacity)
    matrices = near(w_gate, w_up, w_down)
    received = lax.all_to_all(
        packed.reshape(experts, capacity, lanes, 128), "expert", split_axis=0, concat_axis=0, tiled=True
    ).reshape(rows, 2 * slices)

    theirs = theirs_share(received, matrices)
    both = lax.all_gather(
        theirs, "dp", axis=0, tiled=True, axis_index_groups=[[2 * i, 2 * i + 1] for i in range(chips)]
    )
    pair = pair_share(both, received, matrices)
    same_core = [[c + 2 * i for i in range(chips)] for c in range(2)]
    parts = lax.all_to_all(
        pair.reshape(chips, group, 3 * half), "dp", split_axis=0, concat_axis=0, tiled=True,
        axis_index_groups=same_core,
    )
    sums = jnp.sum(parts.astype(F32), axis=0)
    gate, up, hidden_grad = sums[:, :half], sums[:, half : 2 * half], sums[:, 2 * half :]
    hidden_piece = (gate * jax.nn.sigmoid(gate) * up).astype(BF)
    gate_grad_piece, up_grad_piece = gate_grads(hidden_grad, gate, up)
    pieces = jnp.concatenate([hidden_piece, gate_grad_piece, up_grad_piece], axis=1)

    gathered = lax.all_gather(pieces, "dp", axis=0, tiled=True).reshape(chips, 2, group, 3 * half)
    low, high = (gathered[:, c].reshape(rows, 3 * half) for c in range(2))

    packed_back = back_rows(low, high, matrices)
    back = lax.all_to_all(
        packed_back.reshape(experts, capacity, lanes, 128), "expert", split_axis=0, concat_axis=0, tiled=True
    ).reshape(rows, 2 * slices)
    return finish(back, pick, scaled, received, low, high)


def solution(mesh):
    return jax.shard_map(
        local,
        mesh=mesh,
        in_specs=(
            P("expert", "dp"),
            P("expert", None),
            P("expert", None),
            P("expert", "dp", None),
            P("expert", "dp", None),
            P("expert", None, "dp"),
            P("expert", "dp"),
        ),
        out_specs=(
            P("expert", "dp"),
            P("expert", "dp"),
            P("expert", "dp", None),
            P("expert", "dp", None),
            P("expert", None, "dp"),
        ),
        check_vma=False,
    )
```

time: 126 us -> 115 us (0.913)
  blocking collectives: 90.7 us -> 110 us
  waiting for transfers between devices: 17.9 us -> 0 us
  matrix products: 5.17 us -> 0 us
  starting transfers between devices: 4.61 us -> 0 us
  Pallas kernels: 0 us -> 3.91 us
  local copies, waits for them, and re-layouts: 4.06 us -> 0.25 us
  other arithmetic: 2.16 us -> 0.1 us
    all_to_all x1 -> x0, waiting for transfers between devices: 17.9 us -> none  [local(): lax.all_to_all(jnp.concatenate([expert_out, input_rows], axis=1).reshape(...]
    all_to_all x1 -> x2, blocking collectives: 30 us -> 46.8 us  [the longest x1 24.8 us: local(): lax.all_to_all(packed_back.reshape(experts, capacity, lanes, 128), 'exper...]
    dot_general x11 -> x0, matrix products: 5.17 us -> none  [mm(): lax.dot_general(left, right, (((lc,), (rc,)), ((), ())), preferred_elemen...]
    all_to_all x1 -> x0, starting transfers between devices: 4.61 us -> none  [local(): lax.all_to_all(jnp.concatenate([expert_out, input_rows], axis=1).reshape(...]
    pallas_call x0 -> x5, Pallas kernels: none -> 3.91 us  [the longest x1 1.49 us: finish(): pl.pallas_call(finish_body, out_shape=tuple((jax.ShapeDtypeStruct(s, BF)...]
    all_gather x0 -> x1, blocking collectives: none -> 2.44 us  [local(): lax.all_gather(theirs, 'dp', axis=0, tiled=True, axis_index_groups=[[2 *...]
    reshape x4 -> x1, local copies, waits for them, and re-layouts: 2.34 us -> 0.05 us  [local(): packed_back.reshape(experts, capacity, lanes, 128)]
  transfers between devices with their start and end apart: 1 -> 0, of which waited for: 1 -> 0; matrix products, arithmetic and copies ran while one was open for 3% -> 0% of each run, Pallas kernels for 0% -> 0%
where the time goes in v2:
time: 115 us
  blocking collectives  110 us (96%)
  Pallas kernels  3.91 us (3%)
    all_to_all x1, blocking collectives, local(): lax.all_to_all(packed.reshape(experts, capacity, lanes, 128), 'expert', s...  42.4 us
    all_to_all x1, blocking collectives, local(): lax.all_to_all(packed_back.reshape(experts, capacity, lanes, 128), 'exper...  24.8 us
    all_to_all x1, blocking collectives, local(): lax.all_to_all(pair.reshape(chips, group, 3 * half), 'dp', split_axis=0,...  21.9 us
    all_gather x1, blocking collectives, local(): lax.all_gather(pieces, 'dp', axis=0, tiled=True)  18 us
    all_gather x1, blocking collectives, local(): lax.all_gather(theirs, 'dp', axis=0, tiled=True, axis_index_groups=[[2 *...  2.44 us

profile of v2, /device:TPU:8, one launch (start us, length us, event | category | flops | bytes accessed | tf_op | source)
XLA Modules:
  0.0 114.6 jit_solution(369916308280505414)
XLA Ops:
  0.6 1.3 %shard_map.110 = (bf16[192,512]{1,0:T(8,128)(2,1)S(1)}, f32[192,8]{1,0:T(8,128)S(1)}, f32[192,8]{1,0:T(8,128)S(1)}) custom-call(s32[8,8]{1,0:T(8,128)} %refs_0_.1, f32[8,8]{1,0:T(8,128)} %refs_1_.1, bf16[8,256]{1,0:T(8,128)(2,1)} %refs_2_.1, bf16[8,256]{1,0:T(8,128)(2,1)} %refs_3_.1), custom_call_target="tpu_custom_call" | custom-call | tf_op jit(solution)/shard_map/pallas_call | solution.py:56
  1.9 0.0 copy-start.2
  1.9 0.1 reshape.28
  2.0 0.0 copy-start
  2.0 0.0 copy-start.1
  2.0 42.4 %all_to_all.15 = bf16[64,3,4,128]{3,2,1,0:T(4,128)(2,1)S(1)} all-to-all(bf16[64,3,4,128]{3,2,1,0:T(4,128)(2,1)S(1)} %reshape.28), channel_id=1, replica_groups=mesh['dp'=16,'expert'=64] {'expert'}, dimensions={0} | all-to-all | bytes 393216 | tf_op jit(solution)/shard_map/all_to_all | solution.py:209
  44.4 0.0 copy-done.2
  44.4 0.0 copy-done
  44.4 0.0 copy-done.1
  44.4 0.3 shard_map.111
  44.8 2.4 %all_gather.6.both_ref = bf16[384,1152]{1,0:T(8,128)(2,1)S(1)} all-gather(bf16[192,1152]{1,0:T(8,128)(2,1)S(1)} %shard_map.111), channel_id=1, replica_groups={{0,64},{128,192},{256,320},{384,448},{512,576},{640,704},{768,832},{896..., dimensions={0}, use_global_device_ids=true | all-gather | bytes 1327104 | tf_op jit(solution)/shard_map/all_gather | solution.py:214
  47.2 0.3 shard_map.112
  47.5 21.9 %all_to_all.16 = bf16[8,24,1152]{2,1,0:T(8,128)(2,1)S(1)} all-to-all(bf16[8,24,1152]{2,1,0:T(8,128)(2,1)S(1)} %bitcast.21), channel_id=1, replica_groups={{0,128,256,384,512,640,768,896},{64,192,320,448,576,704,832,960},{1,129..., dimensions={0} | all-to-all | bytes 884736 | tf_op jit(solution)/shard_map/all_to_all | solution.py:219
  69.5 0.1 convert_reduce_fusion
  69.6 18.0 %all_gather.7 = bf16[384,1152]{1,0:T(8,128)(2,1)S(1)} all-gather(bf16[24,1152]{1,0:T(8,128)(2,1)S(1)} %pad_maximum_fusion), channel_id=1, replica_groups=mesh['dp'=16,'expert'=64] {'dp'}, dimensions={0}, use_global_device_ids=true | all-gather | bytes 940032 | tf_op jit(solution)/shard_map/all_gather | solution.py:229
  87.6 0.1 fusion.1
  87.7 0.5 shard_map.113
  88.2 0.1 reshape.32
  88.2 24.8 %all_to_all.17 = bf16[64,3,4,128]{3,2,1,0:T(4,128)(2,1)S(1)} all-to-all(bf16[64,3,4,128]{3,2,1,0:T(4,128)(2,1)S(1)} %reshape.32), channel_id=1, replica_groups=mesh['dp'=16,'expert'=64] {'expert'}, dimensions={0} | all-to-all | bytes 393216 | tf_op jit(solution)/shard_map/all_to_all | solution.py:233
  113.1 1.5 %shard_map.114 = (bf16[8,256]{1,0:T(8,128)(2,1)}, bf16[8,256]{1,0:T(8,128)(2,1)}, bf16[1,256,768]{2,1,0:T(8,128)(2,1)}, bf16[1,256,768]{2,1,0:T(8,128)(2,1)}, bf16[1,768,256]{2,1,0:T(8,128)(2,1)}) custom-call(bf16[192,512]{1,0:T(8,128)(2,1)S(1)} %bitcast.22, f32[192,8]{1,0:T(8,128)S(1)} %get-tuple-element.9.pick_ref, ...), custom_call_target="tpu_custom_call" | custom-call | tf_op jit(solution)/shard_map/pallas_call | solution.py:153
  (4 shorter events, 0.1 us)
Async XLA Ops:
  1.9 42.5 %copy-start.2 = (bf16[1,768,256]{2,1,0:T(8,128)(2,1)S(1)}, bf16[1,768,256]{2,1,0:T(8,128)(2,1)}, u32[]{:S(2)}) copy-start(bf16[1,768,256]{2,1,0:T(8,128)(2,1)} %down_ref.5) | copy-start | bytes 1179652
  2.0 42.4 %copy-start = (bf16[1,256,768]{2,1,0:T(8,128)(2,1)S(1)}, bf16[1,256,768]{2,1,0:T(8,128)(2,1)}, u32[]{:S(2)}) copy-start(bf16[1,256,768]{2,1,0:T(8,128)(2,1)} %gate_ref.5) | copy-start | bytes 1179652
  2.0 42.4 %copy-start.1 = (bf16[1,256,768]{2,1,0:T(8,128)(2,1)S(1)}, bf16[1,256,768]{2,1,0:T(8,128)(2,1)}, u32[]{:S(2)}) copy-start(bf16[1,256,768]{2,1,0:T(8,128)(2,1)} %up_ref.5) | copy-start | bytes 1179652

commit v3 on v2

--- a/solution.py
+++ b/solution.py
@@ -110,25 +110,14 @@
     )(*near(both, received), *matrices)
 
 
-def finish_body(
-    back_ref, pick_ref, scaled_ref, rows_ref, low_ref, high_ref, out_ref, in_ref, gate_ref, up_ref, down_ref,
-    out_buf, in_buf, gate_buf, up_buf, down_buf, sems,
-):
+def weight_grads_body(rows_ref, low_ref, high_ref, gate_ref, up_ref, down_ref, gate_buf, up_buf, down_buf, sems):
     width = rows_ref.shape[1] // 2
     half = low_ref.shape[1] // 3
     sides = (low_ref, high_ref)
     expert_in, expert_grad = rows_ref[:, :width], rows_ref[:, width:]
     stores = [
-        pltpu.make_async_copy(buf, out, sems.at[i])
-        for i, (buf, out) in enumerate(
-            (
-                (gate_buf, gate_ref.at[0]),
-                (up_buf, up_ref.at[0]),
-                (down_buf, down_ref.at[0]),
-                (out_buf, out_ref),
-                (in_buf, in_ref),
-            )
-        )
+        pltpu.make_async_copy(buf, out.at[0], sems.at[i])
+        for i, (buf, out) in enumerate(((gate_buf, gate_ref), (up_buf, up_ref), (down_buf, down_ref)))
     ]
     for i, buf in enumerate((gate_buf, up_buf)):
         for c, side in enumerate(sides):
@@ -138,25 +127,33 @@
     for c, side in enumerate(sides):
         down_buf[c * half : (c + 1) * half, :] = dot(side[:, :half], expert_grad, 0, 0).astype(BF)
     stores[2].start()
-    out_buf[...] = dot(scaled_ref[...], back_ref[:, :width].astype(F32), 0, 0, lax.Precision.HIGHEST).astype(BF)
-    stores[3].start()
-    in_buf[...] = dot(pick_ref[...], back_ref[:, width:].astype(F32), 0, 0).astype(BF)
-    stores[4].start()
     for store in stores:
         store.wait()
 
 
-def finish(back, pick, scaled, received, low, high):
+def weight_grads(received, low, high):
     width, half = received.shape[1] // 2, low.shape[1] // 3
-    tok = pick.shape[1]
-    shapes = ((tok, width), (tok, width), (1, width, 2 * half), (1, width, 2 * half), (1, 2 * half, width))
-    return pl.pallas_call(
-        finish_body,
+    shapes = ((1, width, 2 * half), (1, width, 2 * half), (1, 2 * half, width))
+    return pl.pallas_call(
+        weight_grads_body,
         out_shape=tuple(jax.ShapeDtypeStruct(s, BF) for s in shapes),
-        in_specs=[VMEM] * 6,
-        out_specs=(pl.BlockSpec(memory_space=pl.ANY),) * 5,
-        scratch_shapes=[pltpu.VMEM(s[-2:], BF) for s in shapes] + [pltpu.SemaphoreType.DMA((5,))],
-    )(*near(back, pick, scaled, received, low, high))
+        in_specs=[VMEM] * 3,
+        out_specs=(pl.BlockSpec(memory_space=pl.ANY),) * 3,
+        scratch_shapes=[pltpu.VMEM(s[-2:], BF) for s in shapes] + [pltpu.SemaphoreType.DMA((3,))],
+    )(*near(received, low, high))
+
+
+def combine_body(back_ref, pick_ref, scaled_ref, out_ref, in_ref):
+    width = out_ref.shape[1]
+    out_ref[...] = dot(scaled_ref[...], back_ref[:, :width].astype(F32), 0, 0, lax.Precision.HIGHEST).astype(BF)
+    in_ref[...] = dot(pick_ref[...], back_ref[:, width:].astype(F32), 0, 0).astype(BF)
+
+
+def combine(back, pick, scaled):
+    shape = jax.ShapeDtypeStruct((pick.shape[1], back.shape[1] // 2), BF)
+    return pl.pallas_call(
+        combine_body, out_shape=(shape, shape), in_specs=[VMEM] * 3, out_specs=(VMEM, VMEM)
+    )(*near(back, pick, scaled))
 
 
 def back_body(low_ref, high_ref, gate_ref, up_ref, down_ref, rows_ref):
@@ -233,7 +230,8 @@
     back = lax.all_to_all(
         packed_back.reshape(experts, capacity, lanes, 128), "expert", split_axis=0, concat_axis=0, tiled=True
     ).reshape(rows, 2 * slices)
-    return finish(back, pick, scaled, received, low, high)
+    grads = weight_grads(received, low, high)
+    return (*combine(back, pick, scaled), *grads)
 
 
 def solution(mesh):

time: 115 us -> 116 us (level)
  blocking collectives: 110 us -> 84.8 us
  waiting for transfers between devices: 0 us -> 19.6 us
  starting transfers between devices: 0 us -> 4.61 us
    all_to_all x1 -> x0, blocking collectives: 24.8 us -> none  [local(): lax.all_to_all(packed_back.reshape(experts, capacity, lanes, 128), 'exper...]
    all_to_all x0 -> x1, waiting for transfers between devices: none -> 19.6 us  [local(): lax.all_to_all(packed_back.reshape(experts, capacity, lanes, 128), 'exper...]
    all_to_all x0 -> x1, starting transfers between devices: none -> 4.61 us  [local(): lax.all_to_all(packed_back.reshape(experts, capacity, lanes, 128), 'exper...]
  transfers between devices with their start and end apart: 0 -> 1, of which waited for: 0 -> 1; matrix products, arithmetic and copies ran while one was open for 0% -> 0% of each run, Pallas kernels for 0% -> 1%
where the time goes in v3:
time: 116 us; the launch traced here: 115 us
  blocking collectives  84.8 us (73%)
  waiting for transfers between devices  19.6 us (17%)
  Pallas kernels  4.64 us (4%)
  starting transfers between devices  4.61 us (4%)
    all_to_all x1, blocking collectives, local(): lax.all_to_all(packed.reshape(experts, capacity, lanes, 128), 'expert', s...  42.4 us
    all_to_all x1, blocking collectives, local(): lax.all_to_all(pair.reshape(chips, group, 3 * half), 'dp', split_axis=0,...  21.9 us
    all_to_all x1, waiting for transfers between devices, local(): lax.all_to_all(packed_back.reshape(experts, capacity, lanes, 128), 'exper...  19.6 us
    all_gather x1, blocking collectives, local(): lax.all_gather(pieces, 'dp', axis=0, tiled=True)  18 us
    all_to_all x1, starting transfers between devices, local(): lax.all_to_all(packed_back.reshape(experts, capacity, lanes, 128), 'exper...  4.61 us
    all_gather x1, blocking collectives, local(): lax.all_gather(theirs, 'dp', axis=0, tiled=True, axis_index_groups=[[2 *...  2.44 us
  transfers between devices with their start and end apart: 1, of which 1 were waited for; matrix products, arithmetic and copies ran while one was open for 0% of the time, Pallas kernels for 1%

profile of v3, /device:TPU:8, one launch (start us, length us, event | category | flops | bytes accessed | tf_op | source)
XLA Modules:
  0.0 115.4 jit_solution(1945885563817523337)
XLA Ops:
  0.6 1.3 %shard_map.110 = (bf16[192,512]{1,0:T(8,128)(2,1)S(1)}, f32[192,8]{1,0:T(8,128)S(1)}, f32[192,8]{1,0:T(8,128)S(1)}) custom-call(s32[8,8]{1,0:T(8,128)} %refs_0_.1, f32[8,8]{1,0:T(8,128)} %refs_1_.1, bf16[8,256]{1,0:T(8,128)(2,1)} %refs_2_.1, bf16[8,256]{1,0:T(8,128)(2,1)} %refs_3_.1), custom_call_target="tpu_custom_call" | custom-call | tf_op jit(solution)/shard_map/pallas_call | solution.py:56
  1.9 0.0 copy-start.2
  1.9 0.1 reshape.28
  2.0 0.0 copy-start
  2.0 0.0 copy-start.1
  2.0 42.4 %all_to_all.15 = bf16[64,3,4,128]{3,2,1,0:T(4,128)(2,1)S(1)} all-to-all(bf16[64,3,4,128]{3,2,1,0:T(4,128)(2,1)S(1)} %reshape.28), channel_id=1, replica_groups=mesh['dp'=16,'expert'=64] {'expert'}, dimensions={0} | all-to-all | bytes 393216 | tf_op jit(solution)/shard_map/all_to_all | solution.py:206
  44.4 0.0 copy-done.2
  44.4 0.0 copy-done
  44.4 0.0 copy-done.1
  44.4 0.3 shard_map.111
  44.8 2.4 %all_gather.6.both_ref = bf16[384,1152]{1,0:T(8,128)(2,1)S(1)} all-gather(bf16[192,1152]{1,0:T(8,128)(2,1)S(1)} %shard_map.111), channel_id=1, replica_groups={{0,64},{128,192},{256,320},{384,448},{512,576},{640,704},{768,832},{896..., dimensions={0}, use_global_device_ids=true | all-gather | bytes 1327104 | tf_op jit(solution)/shard_map/all_gather | solution.py:211
  47.2 0.3 shard_map.112
  47.5 21.9 %all_to_all.16 = bf16[8,24,1152]{2,1,0:T(8,128)(2,1)S(1)} all-to-all(bf16[8,24,1152]{2,1,0:T(8,128)(2,1)S(1)} %bitcast.21), channel_id=1, replica_groups={{0,128,256,384,512,640,768,896},{64,192,320,448,576,704,832,960},{1,129..., dimensions={0} | all-to-all | bytes 884736 | tf_op jit(solution)/shard_map/all_to_all | solution.py:216
  69.5 0.1 convert_reduce_fusion
  69.6 18.0 %all_gather.7 = bf16[384,1152]{1,0:T(8,128)(2,1)S(1)} all-gather(bf16[24,1152]{1,0:T(8,128)(2,1)S(1)} %pad_maximum_fusion), channel_id=1, replica_groups=mesh['dp'=16,'expert'=64] {'dp'}, dimensions={0}, use_global_device_ids=true | all-gather | bytes 940032 | tf_op jit(solution)/shard_map/all_gather | solution.py:226
  87.6 0.1 fusion.1
  87.7 0.5 shard_map.113
  88.2 0.7 reshape.32
  88.9 4.6 %all-to-all-start.2 = ((bf16[64,3,4,128]{3,2,1,0:T(4,128)(2,1)}), bf16[64,3,4,128]{3,2,1,0:T(4,128)(2,1)S(1)}, u32[]{:S(2)}, u32[]{:S(2)}) async-start(bf16[64,3,4,128]{3,2,1,0:T(4,128)(2,1)} %reshape.32), calls=%async_computation.2 | async-start | bytes 393216 | tf_op jit(solution)/shard_map/all_to_all | solution.py:230
  93.5 1.4 %shard_map.115 = (bf16[1,256,768]{2,1,0:T(8,128)(2,1)}, bf16[1,256,768]{2,1,0:T(8,128)(2,1)}, bf16[1,768,256]{2,1,0:T(8,128)(2,1)}) custom-call(bf16[192,512]{1,0:T(8,128)(2,1)S(1)} %bitcast.20, bf16[192,1152]{1,0:T(8,128)(2,1)S(1)} %bitcast.17, bf16[192,1152]{1,0:T(8,128)(2,1)S(1)} %bitcast.15), custom_call_target="tpu_custom_call" | custom-call | tf_op jit(solution)/shard_map/pallas_call | solution.py:137
  94.9 19.6 %all-to-all-done.2 = bf16[64,3,4,128]{3,2,1,0:T(4,128)(2,1)S(1)} async-done(((bf16[64,3,4,128]{3,2,1,0:T(4,128)(2,1)}), bf16[64,3,4,128]{3,2,1,0:T(4,128)(2,1)S(1)}, u32[]{:S(2)}, u32[]{:S(2)}) %all-to-all-start.2) | async-done | bytes 196640 | tf_op jit(solution)/shard_map/all_to_all | solution.py:230
  114.6 0.9 shard_map.114
  (4 shorter events, 0.1 us)
Async XLA Ops:
  1.9 42.5 %copy-start.2 = (bf16[1,768,256]{2,1,0:T(8,128)(2,1)S(1)}, bf16[1,768,256]{2,1,0:T(8,128)(2,1)}, u32[]{:S(2)}) copy-start(bf16[1,768,256]{2,1,0:T(8,128)(2,1)} %down_ref.5) | copy-start | bytes 1179652
  2.0 42.4 %copy-start = (bf16[1,256,768]{2,1,0:T(8,128)(2,1)S(1)}, bf16[1,256,768]{2,1,0:T(8,128)(2,1)}, u32[]{:S(2)}) copy-start(bf16[1,256,768]{2,1,0:T(8,128)(2,1)} %gate_ref.5) | copy-start | bytes 1179652
  2.0 42.4 %copy-start.1 = (bf16[1,256,768]{2,1,0:T(8,128)(2,1)S(1)}, bf16[1,256,768]{2,1,0:T(8,128)(2,1)}, u32[]{:S(2)}) copy-start(bf16[1,256,768]{2,1,0:T(8,128)(2,1)} %up_ref.5) | copy-start | bytes 1179652
  88.9 25.6 %all-to-all-start.2 = ((bf16[64,3,4,128]{3,2,1,0:T(4,128)(2,1)}), bf16[64,3,4,128]{3,2,1,0:T(4,128)(2,1)S(1)}, u32[]{:S(2)}, u32[]{:S(2)}) async-start(bf16[64,3,4,128]{3,2,1,0:T(4,128)(2,1)} %reshape.32), calls=%async_computation.2 | async-start | bytes 393216 | tf_op jit(solution)/shard_map/all_to_all | solution.py:230
